TPU v7x, 128 devices: a whole 4x4x4 slice. The times are simulated.
128 devices in a mesh: mode: 16 (over z_hi, y, core), gx: 2 (over z_lo), gy: 4 (over x).
Axes of the slice: x: 4, y: 4, z: 4 (z_hi: 2, z_lo: 2; z = z_hi * 2 + z_lo), core: 2. Of those that a mesh axis runs over, the one named last changes fastest.
Arguments:
- right_side: float32 [16, 32, 28672], P('gx', 'gy', 'mode'), may hold values from -6 to 6
- col_block: int32 [224, 32], P('mode'), may hold values from 0 to 223, as said below
- blocks: bfloat16 [224, 32, 128, 128], P('mode'), may hold values from -0.09375 to 0.09375
- relax_rate: float32 [28672], P('mode'), may hold values from 0.5 to 4
- drift_speed: float32 [2, 28672], P(None, 'mode'), may hold values from 0.3 to 1.5
- upwind_sign: int32 [2, 28672], P(None, 'mode'), may hold values from 0 to 1
- wall_mask: int32 [16, 32], P('gx', 'gy'), may hold values 0 or 1
Outputs:
- solution: float32 [16, 32, 28672], P('gx', 'gy', 'mode')
- hessenberg: float32 [4, 3], replicated
Inputs may be any that keep to these rules, and one draw needn't show every extreme that they name: `col_block`: for every block row and every o in 0 .. 15, slots o * 2 to (o + 1) * 2 - 1 hold distinct column blocks of o * 14 to (o + 1) * 14 - 1.
All inputs are finite; a program needn't handle non-finite values. No bound on the sum of `wall_mask` on one device may be relied on, other than what follows from the above.
Results may differ from a plain program's by a relative error of at most 0.00081.
Values may be sent and summed in bfloat16 or wider, within the bound.
A program may use at most 128 MiB of HBM per device.

v0:
```python
import jax
import jax.numpy as jnp
from jax import lax
from jax.sharding import PartitionSpec as P

KRYLOV = 3
epsilon = 1e-12


def extended(block, sides, width):
    for axis, dim in sides:
        count = lax.axis_size(axis)
        forward = [(i, i + 1) for i in range(count - 1)]
        backward = [(target, source) for source, target in forward]
        low = lax.ppermute(
            lax.slice_in_dim(block, block.shape[dim] - width, None, axis=dim), axis, forward
        )
        high = lax.ppermute(lax.slice_in_dim(block, 0, width, axis=dim), axis, backward)
        block = jnp.concatenate([low, block, high], axis=dim)
    return block


def apply_operator(current, col_block, blocks, relax_rate, drift_speed, upwind_sign, open_cells):
    cells_first, cells_second, local_modes = current.shape
    block_size = blocks.shape[2]
    local_blocks = col_block.shape[0]
    slot_count = col_block.shape[1]
    masked = current * open_cells[:, :, None]
    padded = extended(masked, (("gx", 0), ("gy", 1)), 1)
    from_west = padded[:-2, 1:-1]
    from_east = padded[2:, 1:-1]
    from_south = padded[1:-1, :-2]
    from_north = padded[1:-1, 2:]
    upstream_first = jnp.where(upwind_sign[0] == 1, from_west, from_east)
    upstream_second = jnp.where(upwind_sign[1] == 1, from_south, from_north)
    drift_term = drift_speed[0] * (current - upstream_first) + drift_speed[1] * (
        current - upstream_second
    )
    cell_count = cells_first * cells_second
    rounded = current.astype(jnp.bfloat16).reshape(cell_count, local_modes)
    gathered = lax.all_gather(rounded, "mode", axis=1, tiled=True)
    gathered = gathered.reshape(cell_count, -1, block_size)
    picked = jnp.take(gathered, col_block.reshape(-1), axis=1)
    picked = picked.reshape(cell_count, local_blocks, slot_count, block_size)
    scattered = jnp.einsum("rsik,crsk->cri", blocks, picked, preferred_element_type=jnp.float32)
    scattered = scattered.reshape(cells_first, cells_second, local_modes)
    return relax_rate * current + drift_term - scattered


def least_squares(hessenberg, initial):
    upper = [
        [hessenberg[row_index, col_index] for col_index in range(KRYLOV)]
        for row_index in range(KRYLOV + 1)
    ]
    target = [initial] + [jnp.zeros_like(initial) for row_index in range(KRYLOV)]
    cosines = []
    sines = []
    for col_index in range(KRYLOV):
        for row_index in range(col_index):
            first = upper[row_index][col_index]
            second = upper[row_index + 1][col_index]
            upper[row_index][col_index] = cosines[row_index] * first + sines[row_index] * second
            upper[row_index + 1][col_index] = cosines[row_index] * second - sines[row_index] * first
        first = upper[col_index][col_index]
        second = upper[col_index + 1][col_index]
        radius = jnp.sqrt(first * first + second * second)
        cosine = first / radius
        sine_value = second / radius
        upper[col_index][col_index] = radius
        target[col_index + 1] = -sine_value * target[col_index]
        target[col_index] = cosine * target[col_index]
        cosines.append(cosine)
        sines.append(sine_value)
    combo = [None] * KRYLOV
    for row_index in reversed(range(KRYLOV)):
        running = target[row_index]
        for col_index in range(row_index + 1, KRYLOV):
            running = running - upper[row_index][col_index] * combo[col_index]
        combo[row_index] = running / upper[row_index][row_index]
    return combo


def per_device(right_side, col_block, blocks, relax_rate, drift_speed, upwind_sign, wall_mask):
    open_cells = (1 - wall_mask).astype(jnp.float32)
    squared = lax.psum(jnp.sum(right_side * right_side), ("mode", "gx", "gy"))
    initial = jnp.sqrt(squared + epsilon)
    krylov_basis = [right_side / initial]
    columns_list = []
    for section in range(KRYLOV):
        mapped = apply_operator(
            krylov_basis[section],
            col_block,
            blocks,
            relax_rate,
            drift_speed,
            upwind_sign,
            open_cells,
        )
        coefficients = []
        for earlier in range(section + 1):
            projection = lax.psum(jnp.sum(krylov_basis[earlier] * mapped), ("mode", "gx", "gy"))
            mapped = mapped - projection * krylov_basis[earlier]
            coefficients.append(projection)
        length = jnp.sqrt(lax.psum(jnp.sum(mapped * mapped), ("mode", "gx", "gy")) + epsilon)
        krylov_basis.append(mapped / length)
        entries = (
            coefficients
            + [length]
            + [jnp.zeros_like(length) for later in range(KRYLOV - section - 1)]
        )
        columns_list.append(jnp.stack(entries))
    hessenberg = jnp.stack(columns_list, axis=1)
    combo = least_squares(hessenberg, initial)
    solution = jnp.zeros_like(right_side)
    for section in range(KRYLOV):
        solution = solution + combo[section] * krylov_basis[section]
    return (solution, hessenberg)


def solution(mesh):
    return jax.shard_map(
        per_device,
        mesh=mesh,
        in_specs=(
            P("gx", "gy", "mode"),
            P("mode", None),
            P("mode", None, None, None),
            P("mode"),
            P(None, "mode"),
            P(None, "mode"),
            P("gx", "gy"),
        ),
        out_specs=(P("gx", "gy", "mode"), P()),
        check_vma=False,
    )
```

profile of v0, /device:TPU:1, one launch (start us, length us, event | category | flops | bytes accessed | tf_op | source)
XLA Modules:
  0.0 979.8 jit_solution(3949034539014777959)
XLA Ops:
  9.6 68.7 %psum.70 = f32[]{:T(128)} all-reduce(f32[]{:T(128)} %multiply_reduce_fusion.9), channel_id=1, replica_groups=mesh['mode'=16,'gx'=2,'gy'=4] {'mode','gx','gy'}, use_global_device_ids=true, to_apply=%region_1.0 | all-reduce | flops 1 | bytes 8 | tf_op jit(solution)/shard_map/psum | solution.py:85
  82.1 4.0 collective-permute-start
  90.0 4.0 collective-permute-start.2
  94.0 37.7 %all-gather.4.cloned.1.call-done = bf16[64,28672]{1,0:T(8,128)(2,1)} async-done(((bf16[64,1792]{1,0:T(8,128)(2,1)}), bf16[64,28672]{1,0:T(8,128)(2,1)}) %all-gather.4.cloned.1.call-update) | async-done | bytes 3670032 | tf_op jit(solution)/shard_map/all_gather | solution.py:41
  131.8 5.0 copy_bitcast_fusion.2
  136.8 21.7 %gather_fusion = bf16[448,64,128]{2,1,0:T(8,128)(2,1)} fusion(bf16[64,224,128]{2,0,1:T(8,128)(2,1)} %copy_bitcast_fusion.2, s32[1024]{0:T(1024)S(1)} %pad_clamp_fusion), kind=kCustom, calls=%fused_computation.clone | custom fusion | bytes 14681856 | tf_op jit(solution)/shard_map/jit(_take)/gather | solution.py:43
  158.4 7.0 broadcast_select_fusion.2
  165.5 12.4 %convolution_bitcast_fusion.2 = f32[64,14,128]{2,0,1:T(8,128)S(1)} fusion(bf16[64,14,32,128]{3,0,2,1:T(8,128)(2,1)} %bitcast.67, bf16[14,32,128,128]{3,2,1,0:T(8,128)(2,1)} %param.11), kind=kOutput, calls=%fused_computation.11 | convolution fusion | flops 939524096 | bytes 22478848 | tf_op jit(solution)/shard_map/rsik,crsk->cri/dot_general | solution.py:45
  179.2 64.5 %psum.71 = f32[]{:T(128)} all-reduce(f32[]{:T(128)} %get-tuple-element.23), channel_id=1, replica_groups=mesh['mode'=16,'gx'=2,'gy'=4] {'mode','gx','gy'}, use_global_device_ids=true, to_apply=%region_3.5 | all-reduce | flops 1 | bytes 8 | tf_op jit(solution)/shard_map/psum | solution.py:101
  245.1 63.8 %psum.72 = f32[]{:T(128)} all-reduce(f32[]{:T(128)} %multiply_reduce_fusion.7), channel_id=1, replica_groups=mesh['mode'=16,'gx'=2,'gy'=4] {'mode','gx','gy'}, use_global_device_ids=true, to_apply=%region_5.7 | all-reduce | flops 1 | bytes 8 | tf_op jit(solution)/shard_map/psum | solution.py:104
  312.5 4.0 collective-permute-start.4
  319.1 4.0 collective-permute-start.6
  323.1 38.9 %all-gather.6.cloned.1.call-done = bf16[64,28672]{1,0:T(8,128)(2,1)} async-done(((bf16[64,1792]{1,0:T(8,128)(2,1)}), bf16[64,28672]{1,0:T(8,128)(2,1)}) %all-gather.6.cloned.1.call-update) | async-done | bytes 3670032 | tf_op jit(solution)/shard_map/all_gather | solution.py:41
  362.1 5.0 copy_bitcast_fusion.1
  367.1 21.7 %gather_fusion.1 = bf16[448,64,128]{2,1,0:T(8,128)(2,1)} fusion(bf16[64,224,128]{2,0,1:T(8,128)(2,1)} %copy_bitcast_fusion.1, s32[1024]{0:T(1024)S(1)} %pad_clamp_fusion), kind=kCustom, calls=%fused_computation.1.clone | custom fusion | bytes 14681856 | tf_op jit(solution)/shard_map/jit(_take)/gather | solution.py:43
  388.7 7.0 broadcast_select_fusion.1
  395.8 12.3 %convolution_bitcast_fusion.1 = f32[64,14,128]{2,0,1:T(8,128)S(1)} fusion(bf16[64,14,32,128]{3,0,2,1:T(8,128)(2,1)} %bitcast.68, bf16[14,32,128,128]{3,2,1,0:T(8,128)(2,1)} %param.11), kind=kOutput, calls=%fused_computation.10 | convolution fusion | flops 939524096 | bytes 22478848 | tf_op jit(solution)/shard_map/rsik,crsk->cri/dot_general | solution.py:45
  409.4 64.5 %psum.73 = f32[]{:T(128)} all-reduce(f32[]{:T(128)} %get-tuple-element.19), channel_id=1, replica_groups=mesh['mode'=16,'gx'=2,'gy'=4] {'mode','gx','gy'}, use_global_device_ids=true, to_apply=%region_7.9 | all-reduce | flops 1 | bytes 8 | tf_op jit(solution)/shard_map/psum | solution.py:101
  475.3 63.8 %psum.74 = f32[]{:T(128)} all-reduce(f32[]{:T(128)} %multiply_reduce_fusion.5), channel_id=1, replica_groups=mesh['mode'=16,'gx'=2,'gy'=4] {'mode','gx','gy'}, use_global_device_ids=true, to_apply=%region_9.11 | all-reduce | flops 1 | bytes 8 | tf_op jit(solution)/shard_map/psum | solution.py:101
  541.1 62.6 %psum.75 = f32[]{:T(128)} all-reduce(f32[]{:T(128)} %get-tuple-element.17), channel_id=1, replica_groups=mesh['mode'=16,'gx'=2,'gy'=4] {'mode','gx','gy'}, use_global_device_ids=true, to_apply=%region_11.13 | all-reduce | flops 1 | bytes 8 | tf_op jit(solution)/shard_map/psum | solution.py:104
  611.9 4.0 collective-permute-start.8
  618.6 4.0 collective-permute-start.10
  622.6 34.6 %all-gather.8.cloned.1.call-done = bf16[64,28672]{1,0:T(8,128)(2,1)} async-done(((bf16[64,1792]{1,0:T(8,128)(2,1)}), bf16[64,28672]{1,0:T(8,128)(2,1)}) %all-gather.8.cloned.1.call-update) | async-done | bytes 3670032 | tf_op jit(solution)/shard_map/all_gather | solution.py:41
  657.2 5.0 copy_bitcast_fusion
  662.2 21.7 %gather_fusion.2 = bf16[448,64,128]{2,1,0:T(8,128)(2,1)} fusion(bf16[64,224,128]{2,0,1:T(8,128)(2,1)} %copy_bitcast_fusion, s32[1024]{0:T(1024)S(1)} %pad_clamp_fusion), kind=kCustom, calls=%fused_computation.2.clone | custom fusion | bytes 14681856 | tf_op jit(solution)/shard_map/jit(_take)/gather | solution.py:43
  683.9 7.0 broadcast_select_fusion
  690.9 12.3 %convolution_bitcast_fusion = f32[64,14,128]{2,0,1:T(8,128)S(1)} fusion(bf16[64,14,32,128]{3,0,2,1:T(8,128)(2,1)} %bitcast.66, bf16[14,32,128,128]{3,2,1,0:T(8,128)(2,1)} %param.11), kind=kOutput, calls=%fused_computation.9 | convolution fusion | flops 939524096 | bytes 22478848 | tf_op jit(solution)/shard_map/rsik,crsk->cri/dot_general | solution.py:45
  704.6 64.6 %psum.76 = f32[]{:T(128)} all-reduce(f32[]{:T(128)} %get-tuple-element.15), channel_id=1, replica_groups=mesh['mode'=16,'gx'=2,'gy'=4] {'mode','gx','gy'}, use_global_device_ids=true, to_apply=%region_13.15 | all-reduce | flops 1 | bytes 8 | tf_op jit(solution)/shard_map/psum | solution.py:101
  770.5 63.8 %psum.77 = f32[]{:T(128)} all-reduce(f32[]{:T(128)} %multiply_reduce_fusion.2), channel_id=1, replica_groups=mesh['mode'=16,'gx'=2,'gy'=4] {'mode','gx','gy'}, use_global_device_ids=true, to_apply=%region_15.17 | all-reduce | flops 1 | bytes 8 | tf_op jit(solution)/shard_map/psum | solution.py:101
  834.4 2.1 multiply_reduce_fusion.1
  837.8 62.7 %psum.78 = f32[]{:T(128)} all-reduce(f32[]{:T(128)} %get-tuple-element.13), channel_id=1, replica_groups=mesh['mode'=16,'gx'=2,'gy'=4] {'mode','gx','gy'}, use_global_device_ids=true, to_apply=%region_17.19 | all-reduce | flops 1 | bytes 8 | tf_op jit(solution)/shard_map/psum | solution.py:101
  904.2 64.1 %psum.79 = f32[]{:T(128)} all-reduce(f32[]{:T(128)} %multiply_reduce_fusion), channel_id=1, replica_groups=mesh['mode'=16,'gx'=2,'gy'=4] {'mode','gx','gy'}, use_global_device_ids=true, to_apply=%region_19.21 | all-reduce | flops 1 | bytes 8 | tf_op jit(solution)/shard_map/psum | solution.py:104
  (67 shorter events, 35.2 us)
Async XLA Ops:
  7.2 124.6 %all-gather.4.cloned.1.call-start = ((), (), s32[]{:S(2)}) async-start(), calls=%async_computation | async-start | bytes 3899392 | tf_op jit(solution)/shard_map/all_gather | solution.py:41
  80.8 281.3 %all-gather.6.cloned.1.call-start = ((), (), s32[]{:S(2)}) async-start(), calls=%async_computation.1 | async-start | bytes 3899392 | tf_op jit(solution)/shard_map/all_gather | solution.py:41
  80.8 7.8 collective-permute-start.1
  82.1 6.5 collective-permute-start
  88.7 89.5 %collective-permute-start.3 = (f32[10,1,1792]{2,1,0:T(1,128)S(1)}, f32[10,1,1792]{2,1,0:T(1,128)S(1)}, u32[]{:S(2)}, u32[]{:S(2)}) collective-permute-start(f32[10,1,1792]{2,1,0:T(1,128)S(1)} %get-tuple-element.30), channel_id=1, source_target_pairs={{1,0},{2,1},{3,2},{5,4},{6,5},{7,6},{9,8},{10,9},{11,10},{13,12},{... | collective-permute-start | bytes 215048 | tf_op jit(solution)/shard_map/ppermute | solution.py:18
  90.0 88.2 %collective-permute-start.2 = (f32[10,1,1792]{2,1,0:T(1,128)S(1)}, f32[10,1,1792]{2,1,0:T(1,128)S(1)}, u32[]{:S(2)}, u32[]{:S(2)}) collective-permute-start(f32[10,1,1792]{2,1,0:T(1,128)S(1)} %get-tuple-element.29), channel_id=1, source_target_pairs={{0,1},{1,2},{2,3},{4,5},{5,6},{6,7},{8,9},{9,10},{10,11},{12,13},{... | collective-permute-start | bytes 215048 | tf_op jit(solution)/shard_map/ppermute | solution.py:15
  165.5 12.8 %copy-start = (f32[8,8,1792]{2,1,0:T(8,128)S(1)}, f32[8,8,1792]{2,1,0:T(8,128)}, u32[]{:S(2)}) copy-start(f32[8,8,1792]{2,1,0:T(8,128)} %param.9) | copy-start | bytes 1376260
  165.5 12.8 %copy-start.1 = (f32[1792]{0:T(1024)S(1)}, f32[1792]{0:T(1024)}, u32[]{:S(2)}) copy-start(f32[1792]{0:T(1024)} %param.12) | copy-start | bytes 21508
  311.1 346.1 %all-gather.8.cloned.1.call-start = ((), (), s32[]{:S(2)}) async-start(), calls=%async_computation.2 | async-start | bytes 3899392 | tf_op jit(solution)/shard_map/all_gather | solution.py:41
  311.2 5.3 collective-permute-start.5
  312.5 5.2 collective-permute-start.4
  317.8 90.6 %collective-permute-start.7 = (f32[10,1,1792]{2,1,0:T(1,128)S(1)}, f32[10,1,1792]{2,1,0:T(1,128)S(1)}, u32[]{:S(2)}, u32[]{:S(2)}) collective-permute-start(f32[10,1,1792]{2,1,0:T(1,128)S(1)} %get-tuple-element.28), channel_id=1, source_target_pairs={{1,0},{2,1},{3,2},{5,4},{6,5},{7,6},{9,8},{10,9},{11,10},{13,12},{... | collective-permute-start | bytes 215048 | tf_op jit(solution)/shard_map/ppermute | solution.py:18
  319.1 89.3 %collective-permute-start.6 = (f32[10,1,1792]{2,1,0:T(1,128)S(1)}, f32[10,1,1792]{2,1,0:T(1,128)S(1)}, u32[]{:S(2)}, u32[]{:S(2)}) collective-permute-start(f32[10,1,1792]{2,1,0:T(1,128)S(1)} %get-tuple-element.27), channel_id=1, source_target_pairs={{0,1},{1,2},{2,3},{4,5},{5,6},{6,7},{8,9},{9,10},{10,11},{12,13},{... | collective-permute-start | bytes 215048 | tf_op jit(solution)/shard_map/ppermute | solution.py:15
  610.6 6.6 collective-permute-start.9
  611.9 5.3 collective-permute-start.8
  617.3 86.3 %collective-permute-start.11 = (f32[10,1,1792]{2,1,0:T(1,128)S(1)}, f32[10,1,1792]{2,1,0:T(1,128)S(1)}, u32[]{:S(2)}, u32[]{:S(2)}) collective-permute-start(f32[10,1,1792]{2,1,0:T(1,128)S(1)} %get-tuple-element.26), channel_id=1, source_target_pairs={{1,0},{2,1},{3,2},{5,4},{6,5},{7,6},{9,8},{10,9},{11,10},{13,12},{... | collective-permute-start | bytes 215048 | tf_op jit(solution)/shard_map/ppermute | solution.py:18
  618.6 85.0 %collective-permute-start.10 = (f32[10,1,1792]{2,1,0:T(1,128)S(1)}, f32[10,1,1792]{2,1,0:T(1,128)S(1)}, u32[]{:S(2)}, u32[]{:S(2)}) collective-permute-start(f32[10,1,1792]{2,1,0:T(1,128)S(1)} %get-tuple-element.25), channel_id=1, source_target_pairs={{0,1},{1,2},{2,3},{4,5},{5,6},{6,7},{8,9},{9,10},{10,11},{12,13},{... | collective-permute-start | bytes 215048 | tf_op jit(solution)/shard_map/ppermute | solution.py:15
Sparse Core Ops, SparseCore 0:
  80.9 50.8 all-gather.3
  311.3 50.7 all-gather.5
  605.3 51.8 all-gather.7
where the time goes:
time: 992 us; the launch traced here: 980 us
  blocking collectives  643 us (65%)
  waiting for transfers between devices  113 us (11%)
  local copies, waits for them, and re-layouts  83.4 us (8%)
  other arithmetic  45.7 us (5%)
  matrix products  37 us (4%)
  starting transfers between devices  31.8 us (3%)
  between operations  26.1 us (3%)
    psum x6, blocking collectives, per_device(): lax.psum(jnp.sum(krylov_basis[earlier] * mapped), ('mode', 'gx', 'gy'))  384 us
    psum x3, blocking collectives, per_device(): lax.psum(jnp.sum(mapped * mapped), ('mode', 'gx', 'gy')) + epsilon  191 us
    all_gather x3, waiting for transfers between devices, apply_operator(): gathered = lax.all_gather(rounded, 'mode', axis=1, tiled=True)  111 us
    psum x1, blocking collectives, per_device(): squared = lax.psum(jnp.sum(right_side * right_side), ('mode', 'gx', 'gy'))  68.7 us
    gather x3, local copies, waits for them, and re-layouts, apply_operator(): picked = jnp.take(gathered, col_block.reshape(-1), axis=1)  65 us
    dot_general x3, matrix products, apply_operator(): jnp.einsum('rsik,crsk->cri', blocks, picked, preferred_element_type=jnp.f...  37 us
    ppermute x6, starting transfers between devices, extended(): lax.ppermute(lax.slice_in_dim(block, block.shape[dim] - width, None, axis...  23.9 us
    select_n x4, other arithmetic, apply_operator(): picked = jnp.take(gathered, col_block.reshape(-1), axis=1)  21.1 us
  transfers between devices with their start and end apart: 15, of which 4 were waited for; matrix products, arithmetic and copies ran while one was open for 15% of the time, Pallas kernels for 0%

commit v1 on v0

--- a/solution.py
+++ b/solution.py
@@ -5,6 +5,13 @@
 
 KRYLOV = 3
 epsilon = 1e-12
+
+
+def all_by_exchange(x, name, along):
+    size = lax.axis_size(name)
+    tiles = jnp.stack([x for _ in range(size)])
+    tiles = lax.all_to_all(tiles, name, split_axis=0, concat_axis=0)
+    return jnp.concatenate(tiles, axis=along)
 
 
 def extended(block, sides, width):
@@ -38,7 +45,7 @@
     )
     cell_count = cells_first * cells_second
     rounded = current.astype(jnp.bfloat16).reshape(cell_count, local_modes)
-    gathered = lax.all_gather(rounded, "mode", axis=1, tiled=True)
+    gathered = all_by_exchange(rounded, "mode", 1)
     gathered = gathered.reshape(cell_count, -1, block_size)
     picked = jnp.take(gathered, col_block.reshape(-1), axis=1)
     picked = picked.reshape(cell_count, local_blocks, slot_count, block_size)

time: 992 us -> 1030 us (1.038)
  local copies, waits for them, and re-layouts: 83.4 us -> 132 us
  starting transfers between devices: 31.8 us -> 47 us
  between operations: 26.1 us -> 12.8 us
    all_gather x3 -> x0, waiting for transfers between devices: 111 us -> none  [apply_operator(): gathered = lax.all_gather(rounded, 'mode', axis=1, tiled=True)]
    ppermute x6, waiting for transfers between devices: 0.02 us -> 91.2 us  [extended(): lax.ppermute(lax.slice_in_dim(block, 0, width, axis=dim), axis, backward)]
    another operation x1 -> x10, local copies, waits for them, and re-layouts: 0.01 us -> 47.3 us  [the longest x6 40.7 us: apply_operator(): gathered = gathered.reshape(cell_count, -1, block_size)]
    all_to_all x0 -> x3, waiting for transfers between devices: none -> 15.3 us  [all_by_exchange(): tiles = lax.all_to_all(tiles, name, split_axis=0, concat_axis=0)]
    all_to_all x0 -> x3, starting transfers between devices: none -> 15.2 us  [all_by_exchange(): tiles = lax.all_to_all(tiles, name, split_axis=0, concat_axis=0)]
  transfers between devices with their start and end apart: 15 -> 15, of which waited for: 4 -> 6; matrix products, arithmetic and copies ran while one was open for 15% -> 18% of each run, Pallas kernels for 0% -> 0%
where the time goes in v1:
time: 1030 us; the launch traced here: 1020 us
  blocking collectives  643 us (62%)
  local copies, waits for them, and re-layouts  132 us (13%)
  waiting for transfers between devices  106 us (10%)
  starting transfers between devices  47 us (5%)
  other arithmetic  43.9 us (4%)
  matrix products  37 us (4%)
  between operations  12.8 us (1%)
    psum x6, blocking collectives, per_device(): lax.psum(jnp.sum(krylov_basis[earlier] * mapped), ('mode', 'gx', 'gy'))  384 us
    psum x3, blocking collectives, per_device(): lax.psum(jnp.sum(mapped * mapped), ('mode', 'gx', 'gy')) + epsilon  190 us
    ppermute x6, waiting for transfers between devices, extended(): lax.ppermute(lax.slice_in_dim(block, 0, width, axis=dim), axis, backward)  91.2 us
    psum x1, blocking collectives, per_device(): squared = lax.psum(jnp.sum(right_side * right_side), ('mode', 'gx', 'gy'))  68.7 us
    gather x3, local copies, waits for them, and re-layouts, apply_operator(): picked = jnp.take(gathered, col_block.reshape(-1), axis=1)  65 us
    another operation x6, local copies, waits for them, and re-layouts, apply_operator(): gathered = gathered.reshape(cell_count, -1, block_size)  40.7 us
    dot_general x3, matrix products, apply_operator(): jnp.einsum('rsik,crsk->cri', blocks, picked, preferred_element_type=jnp.f...  37 us
    ppermute x6, starting transfers between devices, extended(): lax.ppermute(lax.slice_in_dim(block, block.shape[dim] - width, None, axis...  24.1 us
  transfers between devices with their start and end apart: 15, of which 6 were waited for; matrix products, arithmetic and copies ran while one was open for 18% of the time, Pallas kernels for 0%

profile of v1, /device:TPU:1, one launch (start us, length us, event | category | flops | bytes accessed | tf_op | source)
XLA Modules:
  0.0 1021.9 jit_solution(10276212663221651242)
XLA Ops:
  3.1 68.7 %psum.70 = f32[]{:T(128)} all-reduce(f32[]{:T(128)} %multiply_reduce_fusion.9), channel_id=1, replica_groups=mesh['mode'=16,'gx'=2,'gy'=4] {'mode','gx','gy'}, use_global_device_ids=true, to_apply=%region_1.0 | all-reduce | flops 1 | bytes 8 | tf_op jit(solution)/shard_map/psum | solution.py:92
  75.8 5.2 all-to-all-start
  86.5 32.3 %collective-permute-done.1 = f32[1,8,1792]{2,1,0:T(8,128)S(1)} collective-permute-done((f32[1,8,1792]{2,1,0:T(8,128)S(1)}, f32[1,8,1792]{2,1,0:T(8,128)S(1)}, u32[]{:S(2)}, u32[]{:S(2)}) %collective-permute-start.1) | collective-permute-done | bytes 57376 | tf_op jit(solution)/shard_map/ppermute | solution.py:25
  129.5 5.9 copy.17
  135.4 8.0 reshape_reshape.9
  143.4 5.4 copy.18
  148.7 21.7 %gather_fusion = bf16[448,64,128]{2,1,0:T(8,128)(2,1)} fusion(bf16[64,224,128]{2,0,1:T(8,128)(2,1)} %copy.18, s32[1024]{0:T(1024)S(1)} %pad_clamp_fusion), kind=kCustom, calls=%fused_computation.clone | custom fusion | bytes 14681856 | tf_op jit(solution)/shard_map/jit(_take)/gather | solution.py:50
  170.4 7.2 broadcast_select_fusion.2
  177.7 12.4 %convolution_bitcast_fusion.2 = f32[64,14,128]{2,0,1:T(8,128)S(1)} fusion(bf16[64,14,32,128]{3,0,2,1:T(8,128)(2,1)} %bitcast.55, bf16[14,32,128,128]{3,2,1,0:T(8,128)(2,1)} %param.11), kind=kOutput, calls=%fused_computation.8 | convolution fusion | flops 939524096 | bytes 22478848 | tf_op jit(solution)/shard_map/rsik,crsk->cri/dot_general | solution.py:52
  191.4 64.7 %psum.71 = f32[]{:T(128)} all-reduce(f32[]{:T(128)} %get-tuple-element.23), channel_id=1, replica_groups=mesh['mode'=16,'gx'=2,'gy'=4] {'mode','gx','gy'}, use_global_device_ids=true, to_apply=%region_3.5 | all-reduce | flops 1 | bytes 8 | tf_op jit(solution)/shard_map/psum | solution.py:108
  257.5 63.2 %psum.72 = f32[]{:T(128)} all-reduce(f32[]{:T(128)} %multiply_reduce_fusion.7), channel_id=1, replica_groups=mesh['mode'=16,'gx'=2,'gy'=4] {'mode','gx','gy'}, use_global_device_ids=true, to_apply=%region_5.7 | all-reduce | flops 1 | bytes 8 | tf_op jit(solution)/shard_map/psum | solution.py:111
  334.5 32.7 %collective-permute-done.5 = f32[1,8,1792]{2,1,0:T(8,128)S(1)} collective-permute-done((f32[1,8,1792]{2,1,0:T(8,128)S(1)}, f32[1,8,1792]{2,1,0:T(8,128)S(1)}, u32[]{:S(2)}, u32[]{:S(2)}) %collective-permute-start.5) | collective-permute-done | bytes 57376 | tf_op jit(solution)/shard_map/ppermute | solution.py:25
  377.8 5.9 copy.20
  383.6 8.4 reshape_reshape.10
  392.0 5.4 copy.21
  397.4 21.7 %gather_fusion.1 = bf16[448,64,128]{2,1,0:T(8,128)(2,1)} fusion(bf16[64,224,128]{2,0,1:T(8,128)(2,1)} %copy.21, s32[1024]{0:T(1024)S(1)} %pad_clamp_fusion), kind=kCustom, calls=%fused_computation.1.clone | custom fusion | bytes 14681856 | tf_op jit(solution)/shard_map/jit(_take)/gather | solution.py:50
  419.1 7.2 broadcast_select_fusion.1
  426.2 12.3 %convolution_bitcast_fusion.1 = f32[64,14,128]{2,0,1:T(8,128)S(1)} fusion(bf16[64,14,32,128]{3,0,2,1:T(8,128)(2,1)} %bitcast.56, bf16[14,32,128,128]{3,2,1,0:T(8,128)(2,1)} %param.11), kind=kOutput, calls=%fused_computation.7 | convolution fusion | flops 939524096 | bytes 22478848 | tf_op jit(solution)/shard_map/rsik,crsk->cri/dot_general | solution.py:52
  440.0 64.8 %psum.73 = f32[]{:T(128)} all-reduce(f32[]{:T(128)} %get-tuple-element.19), channel_id=1, replica_groups=mesh['mode'=16,'gx'=2,'gy'=4] {'mode','gx','gy'}, use_global_device_ids=true, to_apply=%region_7.9 | all-reduce | flops 1 | bytes 8 | tf_op jit(solution)/shard_map/psum | solution.py:108
  506.2 63.8 %psum.74 = f32[]{:T(128)} all-reduce(f32[]{:T(128)} %multiply_reduce_fusion.5), channel_id=1, replica_groups=mesh['mode'=16,'gx'=2,'gy'=4] {'mode','gx','gy'}, use_global_device_ids=true, to_apply=%region_9.11 | all-reduce | flops 1 | bytes 8 | tf_op jit(solution)/shard_map/psum | solution.py:108
  572.0 62.6 %psum.75 = f32[]{:T(128)} all-reduce(f32[]{:T(128)} %get-tuple-element.17), channel_id=1, replica_groups=mesh['mode'=16,'gx'=2,'gy'=4] {'mode','gx','gy'}, use_global_device_ids=true, to_apply=%region_11.13 | all-reduce | flops 1 | bytes 8 | tf_op jit(solution)/shard_map/psum | solution.py:111
  654.8 26.2 %collective-permute-done.9 = f32[1,8,1792]{2,1,0:T(8,128)S(1)} collective-permute-done((f32[1,8,1792]{2,1,0:T(8,128)S(1)}, f32[1,8,1792]{2,1,0:T(8,128)S(1)}, u32[]{:S(2)}, u32[]{:S(2)}) %collective-permute-start.9) | collective-permute-done | bytes 57376 | tf_op jit(solution)/shard_map/ppermute | solution.py:25
  691.4 5.9 copy.23
  697.3 8.2 reshape_reshape.11
  705.5 5.4 copy.24
  710.8 21.7 %gather_fusion.2 = bf16[448,64,128]{2,1,0:T(8,128)(2,1)} fusion(bf16[64,224,128]{2,0,1:T(8,128)(2,1)} %copy.24, s32[1024]{0:T(1024)S(1)} %pad_clamp_fusion), kind=kCustom, calls=%fused_computation.2.clone | custom fusion | bytes 14681856 | tf_op jit(solution)/shard_map/jit(_take)/gather | solution.py:50
  732.5 7.3 broadcast_select_fusion
  739.8 12.3 %convolution_bitcast_fusion = f32[64,14,128]{2,0,1:T(8,128)S(1)} fusion(bf16[64,14,32,128]{3,0,2,1:T(8,128)(2,1)} %bitcast.54, bf16[14,32,128,128]{3,2,1,0:T(8,128)(2,1)} %param.11), kind=kOutput, calls=%fused_computation.6 | convolution fusion | flops 939524096 | bytes 22478848 | tf_op jit(solution)/shard_map/rsik,crsk->cri/dot_general | solution.py:52
  753.5 64.5 %psum.76 = f32[]{:T(128)} all-reduce(f32[]{:T(128)} %get-tuple-element.15), channel_id=1, replica_groups=mesh['mode'=16,'gx'=2,'gy'=4] {'mode','gx','gy'}, use_global_device_ids=true, to_apply=%region_13.15 | all-reduce | flops 1 | bytes 8 | tf_op jit(solution)/shard_map/psum | solution.py:108
  819.4 64.0 %psum.77 = f32[]{:T(128)} all-reduce(f32[]{:T(128)} %multiply_reduce_fusion.2), channel_id=1, replica_groups=mesh['mode'=16,'gx'=2,'gy'=4] {'mode','gx','gy'}, use_global_device_ids=true, to_apply=%region_15.17 | all-reduce | flops 1 | bytes 8 | tf_op jit(solution)/shard_map/psum | solution.py:108
  886.8 62.5 %psum.78 = f32[]{:T(128)} all-reduce(f32[]{:T(128)} %get-tuple-element.13), channel_id=1, replica_groups=mesh['mode'=16,'gx'=2,'gy'=4] {'mode','gx','gy'}, use_global_device_ids=true, to_apply=%region_17.19 | all-reduce | flops 1 | bytes 8 | tf_op jit(solution)/shard_map/psum | solution.py:108
  953.1 64.1 %psum.79 = f32[]{:T(128)} all-reduce(f32[]{:T(128)} %multiply_reduce_fusion), channel_id=1, replica_groups=mesh['mode'=16,'gx'=2,'gy'=4] {'mode','gx','gy'}, use_global_device_ids=true, to_apply=%region_19.21 | all-reduce | flops 1 | bytes 8 | tf_op jit(solution)/shard_map/psum | solution.py:111
  (79 shorter events, 87.9 us)
Async XLA Ops:
  0.6 85.6 %copy-start.4 = (s32[14,32]{1,0:T(8,128)S(1)}, s32[14,32]{1,0:T(8,128)}, u32[]{:S(2)}) copy-start(s32[14,32]{1,0:T(8,128)} %param.10) | copy-start | bytes 5380
  0.6 85.7 %copy-start.3 = (f32[2,1792]{1,0:T(2,128)S(1)}, f32[2,1792]{1,0:T(2,128)}, u32[]{:S(2)}) copy-start(f32[2,1792]{1,0:T(2,128)} %param.13) | copy-start | bytes 43012
  0.7 85.7 %copy-start.2 = (s32[2,1792]{1,0:T(2,128)S(1)}, s32[2,1792]{1,0:T(2,128)}, u32[]{:S(2)}) copy-start(s32[2,1792]{1,0:T(2,128)} %param.14) | copy-start | bytes 43012
  75.8 53.7 %all-to-all-start = ((bf16[16,64,1792]{2,1,0:T(8,128)(2,1)}), bf16[16,64,1792]{2,1,0:T(8,128)(2,1)}, u32[]{:S(2)}, u32[]{:S(2)}) async-start(bf16[16,64,1792]{2,1,0:T(8,128)(2,1)} %stack.57), calls=%async_computation | async-start | bytes 7340032 | tf_op jit(solution)/shard_map/all_to_all | solution.py:13
  81.0 37.8 %collective-permute-start.1 = (f32[1,8,1792]{2,1,0:T(8,128)S(1)}, f32[1,8,1792]{2,1,0:T(8,128)S(1)}, u32[]{:S(2)}, u32[]{:S(2)}) collective-permute-start(f32[1,8,1792]{2,1,0:T(8,128)S(1)} %get-tuple-element.38), channel_id=1, source_target_pairs={{4,0},{5,1},{6,2},{7,3},{12,8},{13,9},{14,10},{15,11},{20,16},{21,... | collective-permute-start | bytes 172040 | tf_op jit(solution)/shard_map/ppermute | solution.py:25
  82.3 36.5 %collective-permute-start = (f32[1,8,1792]{2,1,0:T(8,128)S(1)}, f32[1,8,1792]{2,1,0:T(8,128)S(1)}, u32[]{:S(2)}, u32[]{:S(2)}) collective-permute-start(f32[1,8,1792]{2,1,0:T(8,128)S(1)} %get-tuple-element.37), channel_id=1, source_target_pairs={{0,4},{1,5},{2,6},{3,7},{8,12},{9,13},{10,14},{11,15},{16,20},{17,... | collective-permute-start | bytes 172040 | tf_op jit(solution)/shard_map/ppermute | solution.py:22
  118.9 71.5 %collective-permute-start.3 = (f32[10,1,1792]{2,1,0:T(1,128)S(1)}, f32[10,1,1792]{2,1,0:T(1,128)S(1)}, u32[]{:S(2)}, u32[]{:S(2)}) collective-permute-start(f32[10,1,1792]{2,1,0:T(1,128)S(1)} %get-tuple-element.30), channel_id=1, source_target_pairs={{1,0},{2,1},{3,2},{5,4},{6,5},{7,6},{9,8},{10,9},{11,10},{13,12},{... | collective-permute-start | bytes 215048 | tf_op jit(solution)/shard_map/ppermute | solution.py:25
  120.2 70.2 %collective-permute-start.2 = (f32[10,1,1792]{2,1,0:T(1,128)S(1)}, f32[10,1,1792]{2,1,0:T(1,128)S(1)}, u32[]{:S(2)}, u32[]{:S(2)}) collective-permute-start(f32[10,1,1792]{2,1,0:T(1,128)S(1)} %get-tuple-element.29), channel_id=1, source_target_pairs={{0,1},{1,2},{2,3},{4,5},{5,6},{6,7},{8,9},{9,10},{10,11},{12,13},{... | collective-permute-start | bytes 215048 | tf_op jit(solution)/shard_map/ppermute | solution.py:22
  177.6 12.8 %copy-start = (f32[8,8,1792]{2,1,0:T(8,128)S(1)}, f32[8,8,1792]{2,1,0:T(8,128)}, u32[]{:S(2)}) copy-start(f32[8,8,1792]{2,1,0:T(8,128)} %param.9) | copy-start | bytes 1376260
  177.6 12.8 %copy-start.1 = (f32[1792]{0:T(1024)S(1)}, f32[1792]{0:T(1024)}, u32[]{:S(2)}) copy-start(f32[1792]{0:T(1024)} %param.12) | copy-start | bytes 21508
  324.3 53.4 %all-to-all-start.1 = ((bf16[16,64,1792]{2,1,0:T(8,128)(2,1)}), bf16[16,64,1792]{2,1,0:T(8,128)(2,1)}, u32[]{:S(2)}, u32[]{:S(2)}) async-start(bf16[16,64,1792]{2,1,0:T(8,128)(2,1)} %stack.58), calls=%async_computation.1 | async-start | bytes 7340032 | tf_op jit(solution)/shard_map/all_to_all | solution.py:13
  329.2 38.0 %collective-permute-start.5 = (f32[1,8,1792]{2,1,0:T(8,128)S(1)}, f32[1,8,1792]{2,1,0:T(8,128)S(1)}, u32[]{:S(2)}, u32[]{:S(2)}) collective-permute-start(f32[1,8,1792]{2,1,0:T(8,128)S(1)} %get-tuple-element.36), channel_id=1, source_target_pairs={{4,0},{5,1},{6,2},{7,3},{12,8},{13,9},{14,10},{15,11},{20,16},{21,... | collective-permute-start | bytes 172040 | tf_op jit(solution)/shard_map/ppermute | solution.py:25
  330.5 36.7 %collective-permute-start.4 = (f32[1,8,1792]{2,1,0:T(8,128)S(1)}, f32[1,8,1792]{2,1,0:T(8,128)S(1)}, u32[]{:S(2)}, u32[]{:S(2)}) collective-permute-start(f32[1,8,1792]{2,1,0:T(8,128)S(1)} %get-tuple-element.35), channel_id=1, source_target_pairs={{0,4},{1,5},{2,6},{3,7},{8,12},{9,13},{10,14},{11,15},{16,20},{17,... | collective-permute-start | bytes 172040 | tf_op jit(solution)/shard_map/ppermute | solution.py:22
  367.3 71.6 %collective-permute-start.7 = (f32[10,1,1792]{2,1,0:T(1,128)S(1)}, f32[10,1,1792]{2,1,0:T(1,128)S(1)}, u32[]{:S(2)}, u32[]{:S(2)}) collective-permute-start(f32[10,1,1792]{2,1,0:T(1,128)S(1)} %get-tuple-element.28), channel_id=1, source_target_pairs={{1,0},{2,1},{3,2},{5,4},{6,5},{7,6},{9,8},{10,9},{11,10},{13,12},{... | collective-permute-start | bytes 215048 | tf_op jit(solution)/shard_map/ppermute | solution.py:25
  368.6 70.3 %collective-permute-start.6 = (f32[10,1,1792]{2,1,0:T(1,128)S(1)}, f32[10,1,1792]{2,1,0:T(1,128)S(1)}, u32[]{:S(2)}, u32[]{:S(2)}) collective-permute-start(f32[10,1,1792]{2,1,0:T(1,128)S(1)} %get-tuple-element.27), channel_id=1, source_target_pairs={{0,1},{1,2},{2,3},{4,5},{5,6},{6,7},{8,9},{9,10},{10,11},{12,13},{... | collective-permute-start | bytes 215048 | tf_op jit(solution)/shard_map/ppermute | solution.py:22
  637.6 53.8 %all-to-all-start.2 = ((bf16[16,64,1792]{2,1,0:T(8,128)(2,1)}), bf16[16,64,1792]{2,1,0:T(8,128)(2,1)}, u32[]{:S(2)}, u32[]{:S(2)}) async-start(bf16[16,64,1792]{2,1,0:T(8,128)(2,1)} %stack.59), calls=%async_computation.2 | async-start | bytes 7340032 | tf_op jit(solution)/shard_map/all_to_all | solution.py:13
  648.2 32.9 %collective-permute-start.9 = (f32[1,8,1792]{2,1,0:T(8,128)S(1)}, f32[1,8,1792]{2,1,0:T(8,128)S(1)}, u32[]{:S(2)}, u32[]{:S(2)}) collective-permute-start(f32[1,8,1792]{2,1,0:T(8,128)S(1)} %get-tuple-element.32), channel_id=1, source_target_pairs={{4,0},{5,1},{6,2},{7,3},{12,8},{13,9},{14,10},{15,11},{20,16},{21,... | collective-permute-start | bytes 172040 | tf_op jit(solution)/shard_map/ppermute | solution.py:25
  649.5 31.6 %collective-permute-start.8 = (f32[1,8,1792]{2,1,0:T(8,128)S(1)}, f32[1,8,1792]{2,1,0:T(8,128)S(1)}, u32[]{:S(2)}, u32[]{:S(2)}) collective-permute-start(f32[1,8,1792]{2,1,0:T(8,128)S(1)} %get-tuple-element.31), channel_id=1, source_target_pairs={{0,4},{1,5},{2,6},{3,7},{8,12},{9,13},{10,14},{11,15},{16,20},{17,... | collective-permute-start | bytes 172040 | tf_op jit(solution)/shard_map/ppermute | solution.py:22
  681.1 71.3 %collective-permute-start.11 = (f32[10,1,1792]{2,1,0:T(1,128)S(1)}, f32[10,1,1792]{2,1,0:T(1,128)S(1)}, u32[]{:S(2)}, u32[]{:S(2)}) collective-permute-start(f32[10,1,1792]{2,1,0:T(1,128)S(1)} %get-tuple-element.26), channel_id=1, source_target_pairs={{1,0},{2,1},{3,2},{5,4},{6,5},{7,6},{9,8},{10,9},{11,10},{13,12},{... | collective-permute-start | bytes 215048 | tf_op jit(solution)/shard_map/ppermute | solution.py:25
  682.4 70.0 %collective-permute-start.10 = (f32[10,1,1792]{2,1,0:T(1,128)S(1)}, f32[10,1,1792]{2,1,0:T(1,128)S(1)}, u32[]{:S(2)}, u32[]{:S(2)}) collective-permute-start(f32[10,1,1792]{2,1,0:T(1,128)S(1)} %get-tuple-element.25), channel_id=1, source_target_pairs={{0,1},{1,2},{2,3},{4,5},{5,6},{6,7},{8,9},{9,10},{10,11},{12,13},{... | collective-permute-start | bytes 215048 | tf_op jit(solution)/shard_map/ppermute | solution.py:22
